TPU v7x, 32 devices: a whole 2x2x4 slice. The times are simulated.
32 devices in a mesh: light: 4 (over y, x), depth: 2 (over core), height: 4 (over z).
Axes of the slice: x: 2, y: 2, z: 4, core: 2. Of those that a mesh axis runs over, the one named last changes fastest.
Arguments:
- density: float32 [64, 32, 2048], P('light', 'depth', 'height'), may hold values from 0 to 6.4
- active_list: int32 [4, 48], P('depth'), may hold values from -1 to 63, as said below
- light_dir: int32 [8], replicated, may hold values from 0 to 1, as said below
- lamp_plane: float32 [8, 32, 2048], P(None, 'depth', 'height'), may hold values from 0.5 to 2
- extinction: float32 [8], replicated, may hold values from 0.015625 to 0.078125
- blur_weights: float32 [8, 25], replicated, may hold values from 0.2 to 16
- albedo: float32 [8], replicated, may hold values from 0.3 to 1
Outputs:
- rendered: float32 [8, 64, 2048], P('depth', 'light', 'height')
Inputs may be any that keep to these rules, and one draw needn't show every extreme that they name: `active_list`: each row lists distinct brick numbers lb * 16 + hb (lb the light slab of 16 slices, hb the height brick of 128 cells) of one depth slab of 8 cells, then -1 to its end; a row lists between 24 and 48 bricks, and some row lists 48. `light_dir`: exactly 4 entries are 1.
All inputs are finite; a program needn't handle non-finite values.
Results may differ from a plain program's by a relative error of at most 0.00016.
Values sent between devices are 32-bit elements; how exact they have to be, the bound alone decides.
No kernel may reach another device: no remote copies, remote signals or barrier semaphores. Data moves between devices by JAX's collectives and lax.ppermute only.
A program may use at most 64 MiB of HBM per device.

v0:
```python
import jax
import jax.numpy as jnp
from jax import lax
from jax.experimental import pallas as pl
from jax.experimental.pallas import tpu as pltpu
from jax.sharding import PartitionSpec as P

BZ = 8
LANES = 128
TAPS = 5
GRANT = pltpu.CompilerParams(vmem_limit_bytes=24 << 20)
SMEM = pl.BlockSpec(memory_space=pltpu.SMEM)
VMEM = pl.BlockSpec(memory_space=pltpu.VMEM)
HBM = pl.BlockSpec(memory_space=pltpu.HBM)


def pairs_even(count):
    return [(i, i ^ 1) for i in range(count) if (i ^ 1) < count]


def pairs_odd(count):
    inner = [(i, i + 1) for i in range(1, count - 1, 2)]
    return inner + [(b, a) for a, b in inner]


def peer(position, k, count):
    if count & (count - 1) == 0:
        return position ^ k
    return (position - k) % count


def light_pairs(k, count):
    return [(peer(i, k, count), i) for i in range(count)]


def lane_iota(shape):
    return lax.broadcasted_iota(jnp.int32, shape, len(shape) - 1)


def in_vmem(*values):
    return [pltpu.with_memory_space_constraint(v, pltpu.VMEM) for v in values]


def in_hbm(*values):
    return [pltpu.with_memory_space_constraint(v, pltpu.HBM) for v in values]


def in_smem(*values):
    return [pltpu.with_memory_space_constraint(v, pltpu.SMEM) for v in values]


def split(value):
    high = value.astype(jnp.bfloat16)
    return high, (value - high.astype(jnp.float32)).astype(jnp.bfloat16)


def local(density, active_list, light_dir, lamp_plane, extinction, blur_weights, albedo):
    colours = extinction.shape[0]
    slices, depth_len, height_len = density.shape
    chain = lax.axis_size("light")
    groups = lax.axis_size("depth")
    columns = lax.axis_size("height")
    assert groups == 2
    mine = colours // groups
    full = depth_len * groups
    halo = 2 * (chain - 1)
    assert 2 * halo <= LANES
    wide = height_len + LANES
    per_tile = LANES // halo
    tiles = -(-(1 + colours) // per_tile)
    assert 2 * tiles * LANES <= wide * chain
    blocks = height_len // LANES
    slabs = depth_len // BZ
    halo_rows = -(-2 * tiles * LANES // wide) * depth_len

    def place(g):
        return g // per_tile, (g % per_tile) * halo

    def sums_kernel(
        density_hbm, active_hbm, lamp_hbm, dir_hbm, ext_hbm, blur_hbm, albedo_hbm,
        bundle_ref, column_ref, even_ref, odd_ref, dir_ref, ext_ref, blur_ref, albedo_ref,
        density_ref, active_ref, lamp_ref, arrivals,
    ):
        light = lax.axis_index("light")
        depth = lax.axis_index("depth")
        height = lax.axis_index("height")
        moves = [
            pltpu.make_async_copy(source, target, arrivals.at[i])
            for i, (source, target) in enumerate(
                (
                    (density_hbm, density_ref),
                    (active_hbm, active_ref),
                    (lamp_hbm, lamp_ref),
                    (lamp_hbm.at[pl.ds((1 - depth) * mine, mine)], bundle_ref.at[pl.ds(slices, mine)]),
                    (dir_hbm, dir_ref),
                    (ext_hbm, ext_ref),
                    (blur_hbm, blur_ref),
                    (albedo_hbm, albedo_ref),
                )
            )
        ]
        for move in moves:
            move.start()
        moves[1].wait()
        listed = active_ref[...]
        first_brick = (light * columns + height) * blocks
        hits = [
            jnp.max(jnp.where(listed == first_brick + j, 1.0, 0.0), axis=1, keepdims=True)
            for j in range(blocks)
        ]
        moves[0].wait()
        sums = []
        for j, hit in enumerate(hits):
            live = jnp.concatenate(
                [jnp.broadcast_to(hit[r : r + 1], (BZ, LANES)) for r in range(slabs)], axis=0
            )
            span = pl.ds(j * LANES, LANES)
            total = jnp.zeros((depth_len, LANES), jnp.float32)
            for x in range(slices):
                cell = density_ref[x, :, span] * live
                bundle_ref[x, :, span] = cell
                total = total + cell
            column_ref[:, span] = total
            sums.append(total)
        moves[2].wait()
        lane = lane_iota((depth_len, LANES))
        low = [jnp.zeros((depth_len, LANES), jnp.float32) for _ in range(tiles)]
        high = [jnp.zeros((depth_len, LANES), jnp.float32) for _ in range(tiles)]
        for g in range(1 + colours):
            tile, shift = place(g)
            if g == 0:
                left, right = sums[0], sums[-1]
            else:
                owner = depth if g <= mine else 1 - depth
                c = owner * mine + (g - 1) % mine
                left = lamp_ref[c, :, pl.ds(0, LANES)]
                right = lamp_ref[c, :, pl.ds(height_len - LANES, LANES)]
            if shift:
                left = pltpu.roll(left, shift, 1)
                right = pltpu.roll(right, LANES - shift, 1)
            low[tile] = jnp.where((lane >= shift) & (lane < shift + halo), left, low[tile])
            high[tile] = jnp.where(
                (lane >= LANES - shift - halo) & (lane < LANES - shift), right, high[tile]
            )
        even_place = height % 2 == 0
        for t in range(tiles):
            span = pl.ds(t * LANES, LANES)
            even_ref[:, span] = jnp.where(even_place, high[t], low[t])
            odd_ref[:, span] = jnp.where(even_place, low[t], high[t])
        for move in moves[3:]:
            move.wait()

    bundle, column, edge_even, edge_odd, dirs, exts, blurs, albedos = pl.pallas_call(
        sums_kernel,
        name="sums",
        compiler_params=GRANT,
        in_specs=[HBM] * 7,
        out_specs=[VMEM] * 4 + [SMEM] * 4,
        out_shape=(
            pltpu.VMEM((slices + mine, depth_len, height_len), jnp.float32),
            pltpu.VMEM((depth_len, height_len), jnp.float32),
            pltpu.VMEM((depth_len, tiles * LANES), jnp.float32),
            pltpu.VMEM((depth_len, tiles * LANES), jnp.float32),
            pltpu.SMEM(light_dir.shape, jnp.int32),
            pltpu.SMEM(extinction.shape, jnp.float32),
            pltpu.SMEM(blur_weights.shape, jnp.float32),
            pltpu.SMEM(albedo.shape, jnp.float32),
        ),
        scratch_shapes=[
            pltpu.VMEM(density.shape, jnp.float32),
            pltpu.VMEM(active_list.shape, jnp.int32),
            pltpu.VMEM(lamp_plane.shape, jnp.float32),
            pltpu.SemaphoreType.DMA((8,)),
        ],
    )(*in_hbm(density, active_list, lamp_plane, light_dir, extinction, blur_weights, albedo))

    swap = [(0, 1), (1, 0)]
    theirs = lax.ppermute(bundle, "depth", swap)
    got_even = lax.ppermute(edge_even, "height", pairs_even(columns))
    got_odd = lax.ppermute(edge_odd, "height", pairs_odd(columns))

    def gains_body(dir_ref, ext_ref, cells_ref, gain_ref, through_ref, cells, earlier):
        depth = lax.axis_index("depth")
        for j in range(blocks):
            running = jnp.zeros((depth_len, LANES), jnp.float32)
            for x in range(slices):
                rows = pl.ds(x * depth_len, depth_len)
                cell = cells_ref[x, :, pl.ds(j * LANES, LANES)]
                cells[j, rows, :] = cell
                earlier[j, rows, :] = running
                running = running + cell
            earlier[j, pl.ds(slices * depth_len, depth_len), :] = running
        down = [dir_ref[depth * mine + i] == 1 for i in range(mine)]
        rate = [-ext_ref[depth * mine + i] for i in range(mine)]

        def one_depth(z, through):
            passed = []
            for j in range(blocks):
                span = pl.ds(j * LANES, LANES)
                cell = cells[j, pl.ds(z, slices, stride=depth_len), :]
                before_up = earlier[j, pl.ds(z, slices, stride=depth_len), :]
                total = earlier[j, pl.ds(slices * depth_len + z, 1), :]
                before_down = total - before_up - cell
                kept = jnp.exp(cell * (-6.0 / full))
                weight = through[j] * (1.0 - kept)
                for i in range(mine):
                    before = jnp.where(down[i], before_down, before_up)
                    gain_ref[i, z, :, span] = weight * jnp.exp(rate[i] * before)
                passed.append(through[j] * kept)
            return tuple(passed)

        start = tuple(jnp.ones((slices, LANES), jnp.float32) for _ in range(blocks))
        for j, value in enumerate(lax.fori_loop(0, depth_len, one_depth, start)):
            through_ref[:, pl.ds(j * LANES, LANES)] = value

    gains_shape = (
        pltpu.VMEM((mine, depth_len, slices, height_len), jnp.float32),
        pltpu.VMEM((slices, height_len), jnp.float32),
    )
    gains_scratch = [
        pltpu.VMEM((blocks, slices * depth_len, LANES), jnp.float32),
        pltpu.VMEM((blocks, (slices + 1) * depth_len, LANES), jnp.float32),
    ]

    def near_kernel(dir_ref, ext_ref, blur_ref, cells_ref, gain_ref, through_ref, taps_ref, *scratch):
        depth = lax.axis_index("depth")
        shape = (full, LANES)
        lane = lane_iota(shape)
        offset = lane % full - lax.broadcasted_iota(jnp.int32, shape, 0) + TAPS // 2
        for i in range(mine):
            c = depth * mine + i
            norm = blur_ref[c, 0]
            for tap in range(1, TAPS * TAPS):
                norm = norm + blur_ref[c, tap]
            inverse = 1.0 / jnp.full(shape, norm, jnp.float32)
            for b in range(TAPS):
                band = jnp.zeros(shape, jnp.float32)
                for a in range(TAPS):
                    band = jnp.where(offset == a, blur_ref[c, a * TAPS + b], band)
                band = band * inverse
                high = band.astype(jnp.bfloat16).astype(jnp.float32)
                band = jnp.where(lane < 2 * full, high, band - high)
                taps_ref[i, pl.ds(b * full, full), :] = band.astype(jnp.bfloat16)[:, : 3 * full]
        gains_body(dir_ref, ext_ref, cells_ref, gain_ref, through_ref, *scratch)

    gain_near, through_near, taps = pl.pallas_call(
        near_kernel,
        name="near_gains",
        compiler_params=GRANT,
        in_specs=[SMEM] * 3 + [VMEM],
        out_shape=gains_shape + (pltpu.VMEM((mine, TAPS * full, 3 * full), jnp.bfloat16),),
        scratch_shapes=gains_scratch,
    )(*in_smem(dirs, exts, blurs), *in_vmem(bundle))

    def widen_kernel(column_ref, even_ref, odd_ref, wide_ref, halos_ref):
        even_place = lax.axis_index("height") % 2 == 0
        lane = lane_iota((depth_len, LANES))
        for t in range(tiles):
            span = pl.ds(t * LANES, LANES)
            a, b = even_ref[:, span], odd_ref[:, span]
            from_right = jnp.where(even_place, a, b)
            from_left = jnp.where(even_place, b, a)
            halos_ref[:, span] = from_right
            halos_ref[:, pl.ds((tiles + t) * LANES, LANES)] = from_left
            if t == 0:
                edge = jnp.where(
                    lane < halo, from_right, jnp.where(lane >= LANES - halo, from_left, 0.0)
                )
                wide_ref[:, pl.ds(height_len, LANES)] = edge
        wide_ref[:, pl.ds(0, height_len)] = column_ref[...]

    wide_column, halos = pl.pallas_call(
        widen_kernel,
        name="widen",
        compiler_params=GRANT,
        out_shape=(
            pltpu.VMEM((depth_len, wide), jnp.float32),
            pltpu.VMEM((depth_len, 2 * tiles * LANES), jnp.float32),
        ),
    )(*in_vmem(column, got_even, got_odd))

    near = []
    for k in range(1, chain):
        near.append(lax.ppermute(wide_column, "light", light_pairs(k, chain)))

    gain_far, through_far = pl.pallas_call(
        gains_body,
        name="far_gains",
        compiler_params=GRANT,
        in_specs=[SMEM] * 2 + [VMEM],
        out_shape=gains_shape,
        scratch_shapes=gains_scratch,
    )(*in_smem(dirs, exts), *in_vmem(theirs))

    def join_kernel(*refs):
        out_ref = refs[-1]
        for k, ref in enumerate(refs[: chain - 1]):
            out_ref[pl.ds(k * depth_len, depth_len), :] = ref[...]
        for t in range(2 * tiles):
            row, lane = divmod(t * LANES, wide)
            out_ref[pl.ds((chain - 1 + row) * depth_len, depth_len), pl.ds(lane, LANES)] = refs[
                chain - 1
            ][:, pl.ds(t * LANES, LANES)]

    parcel = pl.pallas_call(
        join_kernel,
        name="join",
        compiler_params=GRANT,
        out_shape=pltpu.VMEM(((chain - 1) * depth_len + halo_rows, wide), jnp.float32),
    )(*in_vmem(*near, halos))
    far = lax.ppermute(parcel, "depth", swap)

    def chain_kernel(
        dir_ref, ext_ref, albedo_ref, lamp_ref, theirs_ref, near_ref, far_ref, taps_ref,
        gain_near_ref, through_near_ref, gain_far_ref, through_far_ref, out_ref, walls, plane, lit,
    ):
        light = lax.axis_index("light")
        depth = lax.axis_index("depth")
        height = lax.axis_index("height")
        own_row = pl.multiple_of(depth * depth_len, BZ)
        other_row = pl.multiple_of((1 - depth) * depth_len, BZ)
        for k in range(1, chain):
            source = peer(light, k, chain)
            rows = pl.ds((k - 1) * depth_len, depth_len)
            walls[source, pl.ds(own_row, depth_len), :] = near_ref[rows, :]
            walls[source, pl.ds(other_row, depth_len), :] = far_ref[rows, :]
        lane = lane_iota((depth_len, LANES))

        def halo_tile(ref, t):
            row, first = divmod(t * LANES, wide)
            return ref[pl.ds((chain - 1 + row) * depth_len, depth_len), pl.ds(first, LANES)]

        for i in range(mine):
            for row, group, edges, body in (
                (own_row, 1 + i, near_ref, lamp_ref[depth * mine + i]),
                (other_row, 1 + mine + i, far_ref, theirs_ref[slices + i]),
            ):
                tile, shift = place(group)
                from_right = halo_tile(edges, tile)
                from_left = halo_tile(edges, tiles + tile)
                if shift:
                    from_right = pltpu.roll(from_right, LANES - shift, 1)
                    from_left = pltpu.roll(from_left, shift, 1)
                edge = jnp.where(
                    lane < halo, from_right, jnp.where(lane >= LANES - halo, from_left, 0.0)
                )
                plane[i, pl.ds(row, depth_len), pl.ds(0, height_len)] = body
                plane[i, pl.ds(row, depth_len), pl.ds(height_len, LANES)] = edge
        wide_lane = lane_iota((1, wide))
        inside = (
            (wide_lane < height_len)
            | ((wide_lane < height_len + LANES // 2) & (height < columns - 1))
            | ((wide_lane >= height_len + LANES // 2) & (height > 0))
        )
        inside = jnp.where(inside, 1.0, 0.0)
        down = [dir_ref[depth * mine + i] == 1 for i in range(mine)]
        steps = [jnp.where(d, chain - 1 - light, light) for d in down]
        rate = [-ext_ref[depth * mine + i] for i in range(mine)]

        def one_step(s, carry):
            for i in range(mine):
                wall = walls[jnp.where(down[i], chain - 1 - s, s)]
                before = plane[i]
                high, low = split(before * (jnp.exp(rate[i] * wall) * inside))
                bands = jnp.dot(
                    taps_ref[i],
                    jnp.concatenate([high, low, high], axis=0),
                    preferred_element_type=jnp.float32,
                )
                after = None
                for b in range(TAPS):
                    part = bands[b * full : (b + 1) * full]
                    if b != TAPS // 2:
                        part = pltpu.roll(part, (TAPS // 2 - b) % wide, 1)
                    after = part if after is None else after + part
                plane[i] = jnp.where(s < steps[i], after, before)
            return carry

        lax.fori_loop(0, jnp.maximum(light, chain - 1 - light), one_step, 0)
        in_front = depth == 0
        for i in range(mine):
            for half, row in enumerate((own_row, other_row)):
                lit[half, i] = plane[i, pl.ds(row, depth_len), pl.ds(0, height_len)]
            shade = albedo_ref[depth * mine + i]
            for j in range(blocks):
                span = pl.ds(j * LANES, LANES)
                sums = []
                for half, gain in enumerate((gain_near_ref, gain_far_ref)):
                    parts = [jnp.zeros((slices, LANES), jnp.float32) for _ in range(2)]
                    for z in range(depth_len):
                        light_row = lit[half, i, pl.ds(z, 1), span]
                        parts[z % 2] = parts[z % 2] + light_row * gain[i, z, :, span]
                    sums.append(parts[0] + parts[1])
                front = jnp.where(in_front, sums[0], sums[1])
                back = jnp.where(in_front, sums[1], sums[0])
                through = jnp.where(in_front, through_near_ref[:, span], through_far_ref[:, span])
                out_ref[i, :, span] = shade * (front + through * back)

    return pl.pallas_call(
        chain_kernel,
        name="chain",
        compiler_params=GRANT,
        in_specs=[SMEM] * 3 + [VMEM] * 9,
        out_specs=VMEM,
        out_shape=jax.ShapeDtypeStruct((mine, slices, height_len), jnp.float32),
        scratch_shapes=[
            pltpu.VMEM((chain, full, wide), jnp.float32),
            pltpu.VMEM((mine, full, wide), jnp.float32),
            pltpu.VMEM((groups, mine, depth_len, height_len), jnp.float32),
        ],
    )(
        *in_smem(dirs, exts, albedos),
        *in_vmem(lamp_plane, theirs, parcel, far, taps),
        *in_vmem(gain_near, through_near, gain_far, through_far),
    )


def solution(mesh):
    in_specs = (
        P("light", "depth", "height"),
        P("depth", None),
        P(),
        P(None, "depth", "height"),
        P(),
        P(),
        P(),
    )
    out_specs = P("depth", "light", "height")

    return jax.shard_map(local, mesh=mesh, in_specs=in_specs, out_specs=out_specs, check_vma=False)
```

profile of v0, /device:TPU:17, one launch (start us, length us, event | category | flops | bytes accessed | tf_op | source)
XLA Modules:
  0.0 22.5 jit_solution(282009236943208465)
XLA Ops:
  0.0 0.0 copy-start
  0.0 1.4 %sums.1 = (f32[20,16,512]{2,1,0:T(8,128)S(1)}, f32[16,512]{1,0:T(8,128)S(1)}, f32[16,128]{1,0:T(8,128)S(1)}, f32[16,128]{1,0:T(8,128)S(1)}, s32[8]{0:T(128)S(4)}...) custom-call(f32[16,16,512]{2,1,0:T(8,128)} %density_hbm.1, s32[2,48]{1,0:T(2,128)} %active_hbm.1, ...), custom_call_target="tpu_custom_call" | custom-call | tf_op jit(solution)/shard_map/sums/pallas_call | solution.py:153
  1.4 0.7 %collective-permute-start = (f32[20,16,512]{2,1,0:T(8,128)S(1)}, f32[20,16,512]{2,1,0:T(8,128)S(1)}, u32[]{:S(2)}, u32[]{:S(2)}) collective-permute-start(f32[20,16,512]{2,1,0:T(8,128)S(1)} %get-tuple-element.23.cells_ref), channel_id=1, source_target_pairs={{0,4},{4,0},{1,5},{5,1},{2,6},{6,2},{3,7},{7,3},{8,12},{12,8},{9,1... | collective-permute-start | bytes 1966088 | tf_op jit(solution)/shard_map/ppermute | solution.py:178
  2.1 1.3 %collective-permute-start.1 = (f32[16,128]{1,0:T(8,128)S(1)}, f32[16,128]{1,0:T(8,128)S(1)}, u32[]{:S(2)}, u32[]{:S(2)}) collective-permute-start(f32[16,128]{1,0:T(8,128)S(1)} %get-tuple-element.25), channel_id=1, source_target_pairs={{0,1},{1,0},{2,3},{3,2},{4,5},{5,4},{6,7},{7,6},{8,9},{9,8},{10,11... | collective-permute-start | bytes 24584 | tf_op jit(solution)/shard_map/ppermute | solution.py:179
  3.4 1.9 %collective-permute-start.2 = (f32[16,128]{1,0:T(8,128)S(1)}, f32[16,128]{1,0:T(8,128)S(1)}, u32[]{:S(2)}, u32[]{:S(2)}) collective-permute-start(f32[16,128]{1,0:T(8,128)S(1)} %get-tuple-element.26), channel_id=1, source_target_pairs={{1,2},{2,1},{5,6},{6,5},{9,10},{10,9},{13,14},{14,13},{17,18},{18,... | collective-permute-start | bytes 24584 | tf_op jit(solution)/shard_map/ppermute | solution.py:180
  5.3 0.0 collective-permute-done.1.even_ref
  5.3 2.5 %collective-permute-done.2.odd_ref = f32[16,128]{1,0:T(8,128)S(1)} collective-permute-done((f32[16,128]{1,0:T(8,128)S(1)}, f32[16,128]{1,0:T(8,128)S(1)}, u32[]{:S(2)}, u32[]{:S(2)}) %collective-permute-start.2) | collective-permute-done | bytes 8224 | tf_op jit(solution)/shard_map/ppermute | solution.py:180
  7.8 1.3 %collective-permute-start.3 = (f32[16,640]{1,0:T(8,128)S(1)}, f32[16,640]{1,0:T(8,128)S(1)}, u32[]{:S(2)}, u32[]{:S(2)}) collective-permute-start(f32[16,640]{1,0:T(8,128)S(1)} %get-tuple-element.27), channel_id=1, source_target_pairs={{8,0},{0,8},{24,16},{16,24},{9,1},{1,9},{25,17},{17,25},{10,2},{2,... | collective-permute-start | bytes 122888 | tf_op jit(solution)/shard_map/ppermute | solution.py:284
  9.1 1.2 %collective-permute-start.4 = (f32[16,640]{1,0:T(8,128)S(1)}, f32[16,640]{1,0:T(8,128)S(1)}, u32[]{:S(2)}, u32[]{:S(2)}) collective-permute-start(f32[16,640]{1,0:T(8,128)S(1)} %get-tuple-element.27), channel_id=1, source_target_pairs={{16,0},{24,8},{0,16},{8,24},{17,1},{25,9},{1,17},{9,25},{18,2},{26... | collective-permute-start | bytes 122888 | tf_op jit(solution)/shard_map/ppermute | solution.py:284
  10.3 0.2 collective-permute-start.5
  10.5 0.2 collective-permute-done.3.refs_0_
  10.7 1.2 %collective-permute-done.4.refs_1_ = f32[16,640]{1,0:T(8,128)S(1)} collective-permute-done((f32[16,640]{1,0:T(8,128)S(1)}, f32[16,640]{1,0:T(8,128)S(1)}, u32[]{:S(2)}, u32[]{:S(2)}) %collective-permute-start.4) | collective-permute-done | bytes 40992 | tf_op jit(solution)/shard_map/ppermute | solution.py:284
  11.9 2.2 %collective-permute-done.5.refs_2_ = f32[16,640]{1,0:T(8,128)S(1)} collective-permute-done((f32[16,640]{1,0:T(8,128)S(1)}, f32[16,640]{1,0:T(8,128)S(1)}, u32[]{:S(2)}, u32[]{:S(2)}) %collective-permute-start.5) | collective-permute-done | bytes 40992 | tf_op jit(solution)/shard_map/ppermute | solution.py:284
  14.1 3.2 %collective-permute-start.6 = (f32[64,640]{1,0:T(8,128)S(1)}, f32[64,640]{1,0:T(8,128)S(1)}, u32[]{:S(2)}, u32[]{:S(2)}) collective-permute-start(f32[64,640]{1,0:T(8,128)S(1)} %join.1.near_ref), channel_id=1, source_target_pairs={{0,4},{4,0},{1,5},{5,1},{2,6},{6,2},{3,7},{7,3},{8,12},{12,8},{9,1... | collective-permute-start | bytes 491528 | tf_op jit(solution)/shard_map/ppermute | solution.py:311
  17.4 1.1 %near_gains.1 = (f32[4,16,16,512]{3,2,1,0:T(8,128)S(1)}, f32[16,512]{1,0:T(8,128)S(1)}, bf16[4,160,96]{2,1,0:T(8,128)(2,1)S(1)}) custom-call(s32[8]{0:T(128)S(4)} %get-tuple-element.20.dir_ref, f32[8]{0:T(128)S(4)} %get-tuple-element.21.ext_ref, f32[8,25]{1,0:T(8,128)S(4)} %get-tuple-element.29.blur_ref, f32[20,16,512]{2,1,0:T(8,128)S(1)} %get-tuple-element.23.cells_ref), custom_call_target="tpu_custom_call" | custom-call | tf_op jit(solution)/shard_map/near_gains/pallas_call | solution.py:246
  18.5 0.0 collective-permute-done.cells_ref.theirs_ref
  18.5 0.9 %far_gains.1 = (f32[4,16,16,512]{3,2,1,0:T(8,128)S(1)}, f32[16,512]{1,0:T(8,128)S(1)}) custom-call(s32[8]{0:T(128)S(4)} %get-tuple-element.20.dir_ref, f32[8]{0:T(128)S(4)} %get-tuple-element.21.ext_ref, f32[20,16,512]{2,1,0:T(8,128)S(1)} %collective-permute-done.cells_ref.theirs_ref), custom_call_target="tpu_custom_call" | custom-call | tf_op jit(solution)/shard_map/far_gains/pallas_call | solution.py:286
  19.4 0.0 collective-permute-done.6.far_ref
  19.4 0.0 copy-done
  19.4 3.1 %chain.1 = f32[4,16,512]{2,1,0:T(8,128)} custom-call(s32[8]{0:T(128)S(4)} %get-tuple-element.20.dir_ref, f32[8]{0:T(128)S(4)} %get-tuple-element.21.ext_ref, f32[8]{0:T(128)S(4)} %get-tuple-element.22.albedo_ref, f32[8,16,512]{2,1,0:T(8,128)S(1)} %copy-done, f32[20,16,512]{2,1,0:T(8,128)S(1)} %collective-permute-done.cells_ref.theirs_ref, ...), custom_call_target="tpu_custom_call" | custom-call | tf_op jit(solution)/shard_map/chain/pallas_call | solution.py:399
  (2 shorter events, 0.0 us)
Async XLA Ops:
  0.0 19.4 %copy-start = (f32[8,16,512]{2,1,0:T(8,128)S(1)}, f32[8,16,512]{2,1,0:T(8,128)}, u32[]{:S(2)}) copy-start(f32[8,16,512]{2,1,0:T(8,128)} %lamp_ref.1) | copy-start | bytes 786436
  1.4 17.1 %collective-permute-start = (f32[20,16,512]{2,1,0:T(8,128)S(1)}, f32[20,16,512]{2,1,0:T(8,128)S(1)}, u32[]{:S(2)}, u32[]{:S(2)}) collective-permute-start(f32[20,16,512]{2,1,0:T(8,128)S(1)} %get-tuple-element.23.cells_ref), channel_id=1, source_target_pairs={{0,4},{4,0},{1,5},{5,1},{2,6},{6,2},{3,7},{7,3},{8,12},{12,8},{9,1... | collective-permute-start | bytes 1966088 | tf_op jit(solution)/shard_map/ppermute | solution.py:178
  2.1 3.2 %collective-permute-start.1 = (f32[16,128]{1,0:T(8,128)S(1)}, f32[16,128]{1,0:T(8,128)S(1)}, u32[]{:S(2)}, u32[]{:S(2)}) collective-permute-start(f32[16,128]{1,0:T(8,128)S(1)} %get-tuple-element.25), channel_id=1, source_target_pairs={{0,1},{1,0},{2,3},{3,2},{4,5},{5,4},{6,7},{7,6},{8,9},{9,8},{10,11... | collective-permute-start | bytes 24584 | tf_op jit(solution)/shard_map/ppermute | solution.py:179
  3.4 4.4 %collective-permute-start.2 = (f32[16,128]{1,0:T(8,128)S(1)}, f32[16,128]{1,0:T(8,128)S(1)}, u32[]{:S(2)}, u32[]{:S(2)}) collective-permute-start(f32[16,128]{1,0:T(8,128)S(1)} %get-tuple-element.26), channel_id=1, source_target_pairs={{1,2},{2,1},{5,6},{6,5},{9,10},{10,9},{13,14},{14,13},{17,18},{18,... | collective-permute-start | bytes 24584 | tf_op jit(solution)/shard_map/ppermute | solution.py:180
  7.8 2.9 %collective-permute-start.3 = (f32[16,640]{1,0:T(8,128)S(1)}, f32[16,640]{1,0:T(8,128)S(1)}, u32[]{:S(2)}, u32[]{:S(2)}) collective-permute-start(f32[16,640]{1,0:T(8,128)S(1)} %get-tuple-element.27), channel_id=1, source_target_pairs={{8,0},{0,8},{24,16},{16,24},{9,1},{1,9},{25,17},{17,25},{10,2},{2,... | collective-permute-start | bytes 122888 | tf_op jit(solution)/shard_map/ppermute | solution.py:284
  9.1 2.9 %collective-permute-start.4 = (f32[16,640]{1,0:T(8,128)S(1)}, f32[16,640]{1,0:T(8,128)S(1)}, u32[]{:S(2)}, u32[]{:S(2)}) collective-permute-start(f32[16,640]{1,0:T(8,128)S(1)} %get-tuple-element.27), channel_id=1, source_target_pairs={{16,0},{24,8},{0,16},{8,24},{17,1},{25,9},{1,17},{9,25},{18,2},{26... | collective-permute-start | bytes 122888 | tf_op jit(solution)/shard_map/ppermute | solution.py:284
  10.3 3.8 %collective-permute-start.5 = (f32[16,640]{1,0:T(8,128)S(1)}, f32[16,640]{1,0:T(8,128)S(1)}, u32[]{:S(2)}, u32[]{:S(2)}) collective-permute-start(f32[16,640]{1,0:T(8,128)S(1)} %get-tuple-element.27), channel_id=1, source_target_pairs={{24,0},{16,8},{8,16},{0,24},{25,1},{17,9},{9,17},{1,25},{26,2},{18... | collective-permute-start | bytes 122888 | tf_op jit(solution)/shard_map/ppermute | solution.py:284
  14.1 5.3 %collective-permute-start.6 = (f32[64,640]{1,0:T(8,128)S(1)}, f32[64,640]{1,0:T(8,128)S(1)}, u32[]{:S(2)}, u32[]{:S(2)}) collective-permute-start(f32[64,640]{1,0:T(8,128)S(1)} %join.1.near_ref), channel_id=1, source_target_pairs={{0,4},{4,0},{1,5},{5,1},{2,6},{6,2},{3,7},{7,3},{8,12},{12,8},{9,1... | collective-permute-start | bytes 491528 | tf_op jit(solution)/shard_map/ppermute | solution.py:311
where the time goes:
time: 22.6 us; the launch traced here: 22.5 us
  starting transfers between devices  9.9 us (44%)
  Pallas kernels  6.46 us (29%)
  waiting for transfers between devices  6.06 us (27%)
    ppermute x3, waiting for transfers between devices, local(): near.append(lax.ppermute(wide_column, 'light', light_pairs(k, chain)))  3.6 us
    ppermute x1, starting transfers between devices, local(): far = lax.ppermute(parcel, 'depth', swap)  3.24 us
    pallas_call x1, Pallas kernels, local(): pl.pallas_call(chain_kernel, name='chain', compiler_params=GRANT, in_spec...  3.05 us
    ppermute x3, starting transfers between devices, local(): near.append(lax.ppermute(wide_column, 'light', light_pairs(k, chain)))  2.71 us
    ppermute x1, waiting for transfers between devices, local(): got_odd = lax.ppermute(edge_odd, 'height', pairs_odd(columns))  2.46 us
    ppermute x1, starting transfers between devices, local(): got_odd = lax.ppermute(edge_odd, 'height', pairs_odd(columns))  1.91 us
    pallas_call x1, Pallas kernels, local(): pl.pallas_call(sums_kernel, name='sums', compiler_params=GRANT, in_specs=...  1.37 us
    ppermute x1, starting transfers between devices, local(): got_even = lax.ppermute(edge_even, 'height', pairs_even(columns))  1.3 us
  transfers between devices with their start and end apart: 7, of which 4 were waited for; matrix products, arithmetic and copies ran while one was open for 0% of the time, Pallas kernels for 9%

commit v1 on v0

--- a/solution.py
+++ b/solution.py
@@ -14,13 +14,11 @@
 HBM = pl.BlockSpec(memory_space=pltpu.HBM)
 
 
-def pairs_even(count):
-    return [(i, i ^ 1) for i in range(count) if (i ^ 1) < count]
-
-
-def pairs_odd(count):
-    inner = [(i, i + 1) for i in range(1, count - 1, 2)]
-    return inner + [(b, a) for a, b in inner]
+def swaps(first, count):
+    pairs = {i: i for i in range(count)}
+    for i in range(first, count - 1, 2):
+        pairs[i], pairs[i + 1] = i + 1, i
+    return sorted(pairs.items())
 
 
 def peer(position, k, count):
@@ -176,8 +174,8 @@
 
     swap = [(0, 1), (1, 0)]
     theirs = lax.ppermute(bundle, "depth", swap)
-    got_even = lax.ppermute(edge_even, "height", pairs_even(columns))
-    got_odd = lax.ppermute(edge_odd, "height", pairs_odd(columns))
+    got_even = lax.ppermute(edge_even, "height", swaps(0, columns))
+    got_odd = lax.ppermute(edge_odd, "height", swaps(1, columns))
 
     def gains_body(dir_ref, ext_ref, cells_ref, gain_ref, through_ref, cells, earlier):
         depth = lax.axis_index("depth")

time: 22.6 us -> 22.6 us (level)
  no operation moved by 1% of the time
where the time goes in v1:
time: 22.6 us; the launch traced here: 22.5 us
  starting transfers between devices  9.9 us (44%)
  Pallas kernels  6.46 us (29%)
  waiting for transfers between devices  6.06 us (27%)
    ppermute x3, waiting for transfers between devices, local(): near.append(lax.ppermute(wide_column, 'light', light_pairs(k, chain)))  3.6 us
    ppermute x1, starting transfers between devices, local(): far = lax.ppermute(parcel, 'depth', swap)  3.24 us
    pallas_call x1, Pallas kernels, local(): pl.pallas_call(chain_kernel, name='chain', compiler_params=GRANT, in_spec...  3.05 us
    ppermute x3, starting transfers between devices, local(): near.append(lax.ppermute(wide_column, 'light', light_pairs(k, chain)))  2.71 us
    ppermute x1, waiting for transfers between devices, local(): got_odd = lax.ppermute(edge_odd, 'height', swaps(1, columns))  2.46 us
    ppermute x1, starting transfers between devices, local(): got_odd = lax.ppermute(edge_odd, 'height', swaps(1, columns))  1.91 us
    pallas_call x1, Pallas kernels, local(): pl.pallas_call(sums_kernel, name='sums', compiler_params=GRANT, in_specs=...  1.37 us
    ppermute x1, starting transfers between devices, local(): got_even = lax.ppermute(edge_even, 'height', swaps(0, columns))  1.3 us
  transfers between devices with their start and end apart: 7, of which 4 were waited for; matrix products, arithmetic and copies ran while one was open for 0% of the time, Pallas kernels for 9%

profile of v1, /device:TPU:17, one launch (start us, length us, event | category | flops | bytes accessed | tf_op | source)
XLA Modules:
  0.0 22.5 jit_solution(2713205573457484410)
XLA Ops:
  0.0 0.0 copy-start
  0.0 1.4 %sums.1 = (f32[20,16,512]{2,1,0:T(8,128)S(1)}, f32[16,512]{1,0:T(8,128)S(1)}, f32[16,128]{1,0:T(8,128)S(1)}, f32[16,128]{1,0:T(8,128)S(1)}, s32[8]{0:T(128)S(4)}...) custom-call(f32[16,16,512]{2,1,0:T(8,128)} %density_hbm.1, s32[2,48]{1,0:T(2,128)} %active_hbm.1, ...), custom_call_target="tpu_custom_call" | custom-call | tf_op jit(solution)/shard_map/sums/pallas_call | solution.py:151
  1.4 0.7 %collective-permute-start = (f32[20,16,512]{2,1,0:T(8,128)S(1)}, f32[20,16,512]{2,1,0:T(8,128)S(1)}, u32[]{:S(2)}, u32[]{:S(2)}) collective-permute-start(f32[20,16,512]{2,1,0:T(8,128)S(1)} %get-tuple-element.23.cells_ref), channel_id=1, source_target_pairs={{0,4},{4,0},{1,5},{5,1},{2,6},{6,2},{3,7},{7,3},{8,12},{12,8},{9,1... | collective-permute-start | bytes 1966088 | tf_op jit(solution)/shard_map/ppermute | solution.py:176
  2.1 1.3 %collective-permute-start.1 = (f32[16,128]{1,0:T(8,128)S(1)}, f32[16,128]{1,0:T(8,128)S(1)}, u32[]{:S(2)}, u32[]{:S(2)}) collective-permute-start(f32[16,128]{1,0:T(8,128)S(1)} %get-tuple-element.25), channel_id=1, source_target_pairs={{0,1},{1,0},{2,3},{3,2},{4,5},{5,4},{6,7},{7,6},{8,9},{9,8},{10,11... | collective-permute-start | bytes 24584 | tf_op jit(solution)/shard_map/ppermute | solution.py:177
  3.4 1.9 %collective-permute-start.2 = (f32[16,128]{1,0:T(8,128)S(1)}, f32[16,128]{1,0:T(8,128)S(1)}, u32[]{:S(2)}, u32[]{:S(2)}) collective-permute-start(f32[16,128]{1,0:T(8,128)S(1)} %get-tuple-element.26), channel_id=1, source_target_pairs={{0,0},{1,2},{2,1},{3,3},{4,4},{5,6},{6,5},{7,7},{8,8},{9,10},{10,9... | collective-permute-start | bytes 24584 | tf_op jit(solution)/shard_map/ppermute | solution.py:178
  5.3 0.0 collective-permute-done.1.even_ref
  5.3 2.5 %collective-permute-done.2.odd_ref = f32[16,128]{1,0:T(8,128)S(1)} collective-permute-done((f32[16,128]{1,0:T(8,128)S(1)}, f32[16,128]{1,0:T(8,128)S(1)}, u32[]{:S(2)}, u32[]{:S(2)}) %collective-permute-start.2) | collective-permute-done | bytes 8224 | tf_op jit(solution)/shard_map/ppermute | solution.py:178
  7.8 1.3 %collective-permute-start.3 = (f32[16,640]{1,0:T(8,128)S(1)}, f32[16,640]{1,0:T(8,128)S(1)}, u32[]{:S(2)}, u32[]{:S(2)}) collective-permute-start(f32[16,640]{1,0:T(8,128)S(1)} %get-tuple-element.27), channel_id=1, source_target_pairs={{8,0},{0,8},{24,16},{16,24},{9,1},{1,9},{25,17},{17,25},{10,2},{2,... | collective-permute-start | bytes 122888 | tf_op jit(solution)/shard_map/ppermute | solution.py:282
  9.1 1.2 %collective-permute-start.4 = (f32[16,640]{1,0:T(8,128)S(1)}, f32[16,640]{1,0:T(8,128)S(1)}, u32[]{:S(2)}, u32[]{:S(2)}) collective-permute-start(f32[16,640]{1,0:T(8,128)S(1)} %get-tuple-element.27), channel_id=1, source_target_pairs={{16,0},{24,8},{0,16},{8,24},{17,1},{25,9},{1,17},{9,25},{18,2},{26... | collective-permute-start | bytes 122888 | tf_op jit(solution)/shard_map/ppermute | solution.py:282
  10.3 0.2 collective-permute-start.5
  10.5 0.2 collective-permute-done.3.refs_0_
  10.7 1.2 %collective-permute-done.4.refs_1_ = f32[16,640]{1,0:T(8,128)S(1)} collective-permute-done((f32[16,640]{1,0:T(8,128)S(1)}, f32[16,640]{1,0:T(8,128)S(1)}, u32[]{:S(2)}, u32[]{:S(2)}) %collective-permute-start.4) | collective-permute-done | bytes 40992 | tf_op jit(solution)/shard_map/ppermute | solution.py:282
  11.9 2.2 %collective-permute-done.5.refs_2_ = f32[16,640]{1,0:T(8,128)S(1)} collective-permute-done((f32[16,640]{1,0:T(8,128)S(1)}, f32[16,640]{1,0:T(8,128)S(1)}, u32[]{:S(2)}, u32[]{:S(2)}) %collective-permute-start.5) | collective-permute-done | bytes 40992 | tf_op jit(solution)/shard_map/ppermute | solution.py:282
  14.1 3.2 %collective-permute-start.6 = (f32[64,640]{1,0:T(8,128)S(1)}, f32[64,640]{1,0:T(8,128)S(1)}, u32[]{:S(2)}, u32[]{:S(2)}) collective-permute-start(f32[64,640]{1,0:T(8,128)S(1)} %join.1.near_ref), channel_id=1, source_target_pairs={{0,4},{4,0},{1,5},{5,1},{2,6},{6,2},{3,7},{7,3},{8,12},{12,8},{9,1... | collective-permute-start | bytes 491528 | tf_op jit(solution)/shard_map/ppermute | solution.py:309
  17.4 1.1 %near_gains.1 = (f32[4,16,16,512]{3,2,1,0:T(8,128)S(1)}, f32[16,512]{1,0:T(8,128)S(1)}, bf16[4,160,96]{2,1,0:T(8,128)(2,1)S(1)}) custom-call(s32[8]{0:T(128)S(4)} %get-tuple-element.20.dir_ref, f32[8]{0:T(128)S(4)} %get-tuple-element.21.ext_ref, f32[8,25]{1,0:T(8,128)S(4)} %get-tuple-element.29.blur_ref, f32[20,16,512]{2,1,0:T(8,128)S(1)} %get-tuple-element.23.cells_ref), custom_call_target="tpu_custom_call" | custom-call | tf_op jit(solution)/shard_map/near_gains/pallas_call | solution.py:244
  18.5 0.0 collective-permute-done.cells_ref.theirs_ref
  18.5 0.9 %far_gains.1 = (f32[4,16,16,512]{3,2,1,0:T(8,128)S(1)}, f32[16,512]{1,0:T(8,128)S(1)}) custom-call(s32[8]{0:T(128)S(4)} %get-tuple-element.20.dir_ref, f32[8]{0:T(128)S(4)} %get-tuple-element.21.ext_ref, f32[20,16,512]{2,1,0:T(8,128)S(1)} %collective-permute-done.cells_ref.theirs_ref), custom_call_target="tpu_custom_call" | custom-call | tf_op jit(solution)/shard_map/far_gains/pallas_call | solution.py:284
  19.4 0.0 collective-permute-done.6.far_ref
  19.4 0.0 copy-done
  19.4 3.1 %chain.1 = f32[4,16,512]{2,1,0:T(8,128)} custom-call(s32[8]{0:T(128)S(4)} %get-tuple-element.20.dir_ref, f32[8]{0:T(128)S(4)} %get-tuple-element.21.ext_ref, f32[8]{0:T(128)S(4)} %get-tuple-element.22.albedo_ref, f32[8,16,512]{2,1,0:T(8,128)S(1)} %copy-done, f32[20,16,512]{2,1,0:T(8,128)S(1)} %collective-permute-done.cells_ref.theirs_ref, ...), custom_call_target="tpu_custom_call" | custom-call | tf_op jit(solution)/shard_map/chain/pallas_call | solution.py:397
  (2 shorter events, 0.0 us)
Async XLA Ops:
  0.0 19.4 %copy-start = (f32[8,16,512]{2,1,0:T(8,128)S(1)}, f32[8,16,512]{2,1,0:T(8,128)}, u32[]{:S(2)}) copy-start(f32[8,16,512]{2,1,0:T(8,128)} %lamp_ref.1) | copy-start | bytes 786436
  1.4 17.1 %collective-permute-start = (f32[20,16,512]{2,1,0:T(8,128)S(1)}, f32[20,16,512]{2,1,0:T(8,128)S(1)}, u32[]{:S(2)}, u32[]{:S(2)}) collective-permute-start(f32[20,16,512]{2,1,0:T(8,128)S(1)} %get-tuple-element.23.cells_ref), channel_id=1, source_target_pairs={{0,4},{4,0},{1,5},{5,1},{2,6},{6,2},{3,7},{7,3},{8,12},{12,8},{9,1... | collective-permute-start | bytes 1966088 | tf_op jit(solution)/shard_map/ppermute | solution.py:176
  2.1 3.2 %collective-permute-start.1 = (f32[16,128]{1,0:T(8,128)S(1)}, f32[16,128]{1,0:T(8,128)S(1)}, u32[]{:S(2)}, u32[]{:S(2)}) collective-permute-start(f32[16,128]{1,0:T(8,128)S(1)} %get-tuple-element.25), channel_id=1, source_target_pairs={{0,1},{1,0},{2,3},{3,2},{4,5},{5,4},{6,7},{7,6},{8,9},{9,8},{10,11... | collective-permute-start | bytes 24584 | tf_op jit(solution)/shard_map/ppermute | solution.py:177
  3.4 4.4 %collective-permute-start.2 = (f32[16,128]{1,0:T(8,128)S(1)}, f32[16,128]{1,0:T(8,128)S(1)}, u32[]{:S(2)}, u32[]{:S(2)}) collective-permute-start(f32[16,128]{1,0:T(8,128)S(1)} %get-tuple-element.26), channel_id=1, source_target_pairs={{0,0},{1,2},{2,1},{3,3},{4,4},{5,6},{6,5},{7,7},{8,8},{9,10},{10,9... | collective-permute-start | bytes 24584 | tf_op jit(solution)/shard_map/ppermute | solution.py:178
  7.8 2.9 %collective-permute-start.3 = (f32[16,640]{1,0:T(8,128)S(1)}, f32[16,640]{1,0:T(8,128)S(1)}, u32[]{:S(2)}, u32[]{:S(2)}) collective-permute-start(f32[16,640]{1,0:T(8,128)S(1)} %get-tuple-element.27), channel_id=1, source_target_pairs={{8,0},{0,8},{24,16},{16,24},{9,1},{1,9},{25,17},{17,25},{10,2},{2,... | collective-permute-start | bytes 122888 | tf_op jit(solution)/shard_map/ppermute | solution.py:282
  9.1 2.9 %collective-permute-start.4 = (f32[16,640]{1,0:T(8,128)S(1)}, f32[16,640]{1,0:T(8,128)S(1)}, u32[]{:S(2)}, u32[]{:S(2)}) collective-permute-start(f32[16,640]{1,0:T(8,128)S(1)} %get-tuple-element.27), channel_id=1, source_target_pairs={{16,0},{24,8},{0,16},{8,24},{17,1},{25,9},{1,17},{9,25},{18,2},{26... | collective-permute-start | bytes 122888 | tf_op jit(solution)/shard_map/ppermute | solution.py:282
  10.3 3.8 %collective-permute-start.5 = (f32[16,640]{1,0:T(8,128)S(1)}, f32[16,640]{1,0:T(8,128)S(1)}, u32[]{:S(2)}, u32[]{:S(2)}) collective-permute-start(f32[16,640]{1,0:T(8,128)S(1)} %get-tuple-element.27), channel_id=1, source_target_pairs={{24,0},{16,8},{8,16},{0,24},{25,1},{17,9},{9,17},{1,25},{26,2},{18... | collective-permute-start | bytes 122888 | tf_op jit(solution)/shard_map/ppermute | solution.py:282
  14.1 5.3 %collective-permute-start.6 = (f32[64,640]{1,0:T(8,128)S(1)}, f32[64,640]{1,0:T(8,128)S(1)}, u32[]{:S(2)}, u32[]{:S(2)}) collective-permute-start(f32[64,640]{1,0:T(8,128)S(1)} %join.1.near_ref), channel_id=1, source_target_pairs={{0,4},{4,0},{1,5},{5,1},{2,6},{6,2},{3,7},{7,3},{8,12},{12,8},{9,1... | collective-permute-start | bytes 491528 | tf_op jit(solution)/shard_map/ppermute | solution.py:309
